TPU v7x, 256 devices: a whole 4x4x8 slice. The times are simulated.
256 devices in a mesh: crop: 2 (over y_hi), rows: 16 (over y_lo, x, core), hid: 8 (over z).
Axes of the slice: x: 4, y: 4 (y_hi: 2, y_lo: 2; y = y_hi * 2 + y_lo), z: 8, core: 2. Of those that a mesh axis runs over, the one named last changes fastest.
Arguments:
- tokens: bfloat16 [2, 32, 64, 4096], P('crop', 'rows', None, 'hid'), may hold values from -6 to 6
- cotangent: bfloat16 [2, 32, 64, 4096], P('crop', 'rows', None, 'hid'), may hold values from -6 to 6
- weight_in: bfloat16 [256, 64, 5, 256], P('rows', 'hid'), may hold values from -0.15625 to 0.15625
- weight_out: bfloat16 [256, 64, 5, 256], P('rows', 'hid'), may hold values from -0.078125 to 0.078125
- mix_kernel: float32 [9, 16384], P(None, 'hid'), may hold values from -4 to 4
- block_rows: int32 [64, 5], P('hid'), may hold values from 0 to 15, as said below
Outputs:
- grad_tokens: bfloat16 [2, 32, 64, 4096], P('crop', 'rows', None, 'hid')
- grad_w_in: float32 [256, 64, 5, 256], P(('crop', 'rows'), 'hid')
- grad_w_out: float32 [256, 64, 5, 256], P(('crop', 'rows'), 'hid')
- grad_kernel: float32 [9, 16384], P(None, 'hid')
Inputs may be any that keep to these rules, and one draw needn't show every extreme that they name: In each block column c, block_rows[c, 0] is a label L and block_rows[c, k] for k >= 1 is L with bit k - 1 flipped, so the 5 entries of a column differ; every value is the label of equally many block columns.
All inputs are finite; a program needn't handle non-finite values.
Results may differ from a plain program's by a relative error of at most 0.019.
Values may be sent and summed in bfloat16 or wider, within the bound.
No kernel may reach another device: no remote copies, remote signals or barrier semaphores. Data moves between devices by JAX's collectives and lax.ppermute only.
A program may use at most 128 MiB of HBM per device.

v0:
```python
import jax
import jax.numpy as jnp
from jax import lax
from jax.sharding import PartitionSpec as P

root_two_pi = 0.7978845608
cubic_coef = 0.044715
loss_scale = 0.03125


def padded(shard, sides, width):
    for axis, dim in sides:
        devices, length = (lax.axis_size(axis), shard.shape[dim])
        up = [(i, (i + 1) % devices) for i in range(devices - 1)]
        down = [(j, i) for i, j in up]
        last = lax.slice_in_dim(shard, length - width, length, axis=dim)
        initial = lax.slice_in_dim(shard, 0, width, axis=dim)
        before = lax.ppermute(last, axis, up)
        after = lax.ppermute(initial, axis, down)
        shard = jnp.concatenate([before, shard, after], axis=dim)
    return shard


def gelu_pair(preact):
    inner = root_two_pi * (preact + cubic_coef * preact * preact * preact)
    tanh_val = jnp.tanh(inner)
    gelu_out = 0.5 * preact * (1.0 + tanh_val)
    slopes = 0.5 * (1.0 + tanh_val) + 0.5 * preact * (1.0 - tanh_val * tanh_val) * root_two_pi * (
        1.0 + 3.0 * cubic_coef * preact * preact
    )
    return (gelu_out, slopes)


def on_device(tokens, cotangent, weight_in, weight_out, mix_kernel, block_rows):
    in_panel, out_panel = (
        lax.all_gather(weight_in, "rows", axis=0, tiled=True),
        lax.all_gather(weight_out, "rows", axis=0, tiled=True),
    )
    tok_full, cot_full = (
        lax.all_gather(tokens, "hid", axis=3, tiled=True),
        lax.all_gather(cotangent, "hid", axis=3, tiled=True),
    )
    crop_count, height, grid_width, depth_all = tok_full.shape
    tok_count = crop_count * height * grid_width
    block_size = in_panel.shape[0]
    col_count = in_panel.shape[1]
    nnz_count = in_panel.shape[2]
    block_count = depth_all // block_size
    hidden_local = col_count * block_size
    flat_rows = block_rows.reshape(-1)
    in_select = jnp.take(
        tok_full.reshape(tok_count, block_count, block_size), flat_rows, axis=1
    ).reshape(tok_count, col_count, nnz_count, block_size)
    grad_select = jnp.take(
        cot_full.reshape(tok_count, block_count, block_size), flat_rows, axis=1
    ).reshape(tok_count, col_count, nnz_count, block_size)
    pre_act = jnp.einsum("tckb,bcke->tce", in_select, in_panel, preferred_element_type=jnp.float32)
    gelu_out, slopes = gelu_pair(pre_act)
    active = gelu_out.astype(jnp.bfloat16).reshape(crop_count, height, grid_width, hidden_local)
    act_rim = padded(active, (("rows", 1),), 1)
    mix_grad = (
        jnp.einsum("tckd,fckd->tcf", grad_select, out_panel, preferred_element_type=jnp.float32)
        .astype(jnp.bfloat16)
        .reshape(crop_count, height, grid_width, hidden_local)
    )
    grad_rim = padded(mix_grad, (("rows", 1),), 1)
    act_pad = jnp.pad(act_rim.astype(jnp.float32), ((0, 0), (0, 0), (1, 1), (0, 0)))
    grad_pad = jnp.pad(grad_rim.astype(jnp.float32), ((0, 0), (0, 0), (1, 1), (0, 0)))
    grad_grid = mix_grad.astype(jnp.float32)
    mix_sum = jnp.zeros((crop_count, height, grid_width, hidden_local), jnp.float32)
    act_grad = jnp.zeros((crop_count, height, grid_width, hidden_local), jnp.float32)
    kern_terms = []
    for row_off in range(3):
        for col_off in range(3):
            tap = mix_kernel[3 * row_off + col_off]
            shifted = act_pad[:, row_off : row_off + height, col_off : col_off + grid_width]
            mix_sum = mix_sum + tap * shifted
            act_grad = (
                act_grad
                + tap
                * grad_pad[
                    :, 2 - row_off : 2 - row_off + height, 2 - col_off : 2 - col_off + grid_width
                ]
            )
            kern_terms.append(jnp.sum(shifted * grad_grid, axis=(0, 1, 2)))
    kern_local = jnp.stack(kern_terms, axis=0) * loss_scale
    mix_out = mix_sum.astype(jnp.bfloat16).reshape(tok_count, col_count, block_size)
    pre_grad = (act_grad.reshape(tok_count, col_count, block_size) * slopes).astype(jnp.bfloat16)
    kern_total = lax.psum(kern_local.astype(jnp.bfloat16), ("crop", "rows")).astype(jnp.float32)
    back_select = jnp.einsum(
        "tce,bcke->tckb", pre_grad, in_panel, preferred_element_type=jnp.float32
    )
    one_hot = (
        block_rows[:, :, None] == jnp.arange(block_count, dtype=jnp.int32)[None, None, :]
    ).astype(jnp.float32)
    token_terms = jnp.einsum(
        "tckb,ckr->trb", back_select, one_hot, precision=lax.Precision.HIGHEST
    ).reshape(crop_count, height, grid_width, depth_all)
    grad_tokens = lax.psum_scatter(
        token_terms.astype(jnp.bfloat16), "hid", scatter_dimension=3, tiled=True
    )
    first_term = jnp.einsum(
        "tckb,tce->bcke", in_select, pre_grad, preferred_element_type=jnp.float32
    )
    second_term = jnp.einsum(
        "tcf,tckd->fckd", mix_out, grad_select, preferred_element_type=jnp.float32
    )
    share_sums = lax.psum_scatter(
        (jnp.stack([first_term, second_term], axis=1) * loss_scale).astype(jnp.bfloat16),
        ("crop", "rows"),
        scatter_dimension=0,
        tiled=True,
    ).astype(jnp.float32)
    return (grad_tokens, share_sums[:, 0], share_sums[:, 1], kern_total)


def solution(mesh):
    placed = (
        P("crop", "rows", None, "hid"),
        P("crop", "rows", None, "hid"),
        P("rows", "hid", None, None),
        P("rows", "hid", None, None),
        P(None, "hid"),
        P("hid", None),
    )
    return jax.shard_map(
        on_device,
        mesh=mesh,
        in_specs=placed,
        out_specs=(
            P("crop", "rows", None, "hid"),
            P(("crop", "rows"), "hid", None, None),
            P(("crop", "rows"), "hid", None, None),
            P(None, "hid"),
        ),
        check_vma=False,
    )
```

profile of v0, /device:TPU:4, one launch (start us, length us, event | category | flops | bytes accessed | tf_op | source)
XLA Modules:
  0.0 380.4 jit_solution(11429003799002727429)
XLA Ops:
  7.2 0.7 all-gather.9.cloned.1.call-update
  7.9 0.7 all-gather.5.cloned.1.call-update
  8.7 1.8 copy.46
  10.5 1.8 copy.49
  12.4 0.8 reshape.183
  13.2 38.3 %all-gather.9.cloned.1.call-done = bf16[1,2,64,4096]{3,2,1,0:T(8,128)(2,1)} async-done(((bf16[1,2,64,512]{3,2,1,0:T(8,128)(2,1)}), bf16[1,2,64,4096]{3,2,1,0:T(8,128)(2,1)}) %all-gather.9.cloned.1.call-update) | async-done | bytes 1048592 | tf_op jit(solution)/shard_map/all_gather | solution.py:40
  51.5 1.5 copy.70
  53.0 0.3 copy.48
  53.3 37.1 %all-gather.5.cloned.1.call-done = bf16[1,2,64,4096]{3,2,1,0:T(8,128)(2,1)} async-done(((bf16[1,2,64,512]{3,2,1,0:T(8,128)(2,1)}), bf16[1,2,64,4096]{3,2,1,0:T(8,128)(2,1)}) %all-gather.5.cloned.1.call-update) | async-done | bytes 1048592 | tf_op jit(solution)/shard_map/all_gather | solution.py:41
  90.4 1.5 copy.68
  91.9 0.3 copy.45
  92.2 2.4 gather_fusion.1
  94.6 2.4 gather_fusion
  97.0 4.6 %broadcast_select_fusion.1 = (bf16[40,128,256]{2,1,0:T(8,128)(2,1)S(1)}, bf16[40,128,256]{2,1,0:T(8,128)(2,1)}) fusion(bf16[40,128,256]{2,1,0:T(8,128)(2,1)} %gather_fusion, pred[40]{0:T(512)(128)(4,1)S(1)} %compare_and_fusion, bf16[40,128,256]{2,1,0:T(8,128)(2,1)} %gather_fusion.1), kind=kLoop, calls=%fused_computation.18 | loop fusion | flops 2621440 | bytes 10485800 | tf_op jit(solution)/shard_map/jit(_take)/select_n | solution.py:54
  101.6 30.2 %all-gather.7.cloned.1.call-done = bf16[256,8,5,256]{3,0,2,1:T(8,128)(2,1)} async-done(((bf16[16,8,5,256]{3,0,2,1:T(8,128)(2,1)}), bf16[256,8,5,256]{3,0,2,1:T(8,128)(2,1)}) %all-gather.7.cloned.1.call-update) | async-done | bytes 5242896 | tf_op jit(solution)/shard_map/all_gather | solution.py:37
  131.8 4.3 %fusion.9 = bf16[128,8,256]{2,0,1:T(8,128)(2,1)S(1)} fusion(bf16[128,8,5,256]{3,0,2,1:T(8,128)(2,1)S(1)} %bitcast.97, bf16[256,8,5,256]{3,0,2,1:T(8,128)(2,1)} %all-gather.7.cloned.1.call-done), kind=kOutput, calls=%fused_computation.39 | convolution fusion | flops 671350784 | bytes 8388608 | tf_op jit(solution)/shard_map/tckd,fckd->tcf/dot_general | solution.py:62
  136.2 1.1 copy.47
  137.2 1.3 reshape.185
  138.6 2.1 collective-permute-start
  140.7 3.4 collective-permute-start.1
  144.2 2.0 collective-permute-done
  146.3 3.6 collective-permute-done.1
  150.0 0.9 fusion.25
  150.9 1.3 copy.69
  152.2 25.9 %all-gather.11.cloned.1.call-done = bf16[256,8,5,256]{3,0,2,1:T(8,128)(2,1)} async-done(((bf16[16,8,5,256]{3,0,2,1:T(8,128)(2,1)}), bf16[256,8,5,256]{3,0,2,1:T(8,128)(2,1)}) %all-gather.11.cloned.1.call-update) | async-done | bytes 5242896 | tf_op jit(solution)/shard_map/all_gather | solution.py:36
  178.1 5.1 %multiply_convert_fusion = (bf16[128,8,256]{2,0,1:T(8,128)(2,1)S(1)}, bf16[128,8,256]{2,0,1:T(8,128)(2,1)}) fusion(f32[128,8,256]{2,1,0:T(8,128)} %bitcast.108, bf16[128,8,5,256]{3,0,2,1:T(8,128)(2,1)S(1)} %bitcast.99, bf16[256,8,5,256]{3,0,2,1:T(8,128)(2,1)} %all-gather.11.cloned.1.call-done), kind=kOutput, calls=%fused_computation.76 | convolution fusion | flops 676593664 | bytes 9961472 | tf_op jit(solution)/shard_map/tckb,bcke->tce/dot_general | solution.py:57
  183.3 1.1 copy.53
  184.4 2.1 reshape.189
  186.5 1.1 fusion.46
  187.5 2.1 collective-permute-start.2
  189.7 3.6 collective-permute-start.3
  193.3 2.7 convolution_bitcast_fusion.1
  196.0 1.0 collective-permute-done.3
  197.2 0.9 add_convert_fusion
  198.2 0.7 copy-done.1
  198.9 1.6 convolution_bitcast_fusion
  200.5 5.7 %fusion = bf16[256,2,8,5,256]{0,4,3,2,1:T(8,128)(2,1)} fusion(f32[256,1,8,5,256]{0,4,3,2,1:T(8,128)S(1)} %convolution_bitcast_fusion, f32[256,1,8,5,256]{0,4,3,2,1:T(8,128)S(1)} %convolution_bitcast_fusion.1), kind=kLoop, calls=%fused_computation.3 | loop fusion | flops 15728640 | bytes 31457280 | tf_op jit(solution)/shard_map/convert_element_type | solution.py:109
  206.2 15.4 %copy.56 = bf16[256,2,8,5,256]{4,2,3,1,0:T(8,128)(2,1)} copy(bf16[256,2,8,5,256]{0,4,3,2,1:T(8,128)(2,1)} %fusion) | data formatting | bytes 20971520 | tf_op jit(solution)/shard_map/convert_element_type | solution.py:109
  221.9 0.4 copy-done.6
  222.6 4.3 %convolution_bitcast_fusion.2 = f32[128,8,5,256]{3,0,2,1:T(8,128)S(1)} fusion(bf16[256,8,5,256]{3,0,2,1:T(8,128)(2,1)} %all-gather.11.cloned.1.call-done, bf16[128,8,256]{2,0,1:T(8,128)(2,1)S(1)} %copy-done.4), kind=kOutput, calls=%fused_computation.19 | convolution fusion | flops 671088640 | bytes 11010048 | tf_op jit(solution)/shard_map/tce,bcke->tckb/dot_general | solution.py:90
  227.0 5.9 %fusion.5 = bf16[128,16,256]{2,1,0:T(8,128)(2,1)} fusion(f32[128,8,5,256]{3,0,2,1:T(8,128)S(1)} %convolution_bitcast_fusion.2, s32[8,5]{0,1:T(8,128)S(1)} %copy.44), kind=kOutput, calls=%fused_computation.35 | convolution fusion | flops 252183168 | bytes 6291616 | tf_op jit(solution)/shard_map/tckb,ckr->trb/dot_general | solution.py:96
  232.8 2.3 convert_element_type.87
  235.2 1.0 fusion.39
  236.4 117.1 %psum.7 = bf16[9,2048]{1,0:T(8,128)(2,1)S(1)} all-reduce(bf16[9,2048]{1,0:T(8,128)(2,1)S(1)} %multiply_convert_fusion.1), channel_id=1, replica_groups=mesh['crop'=2,'rows'=16,'hid'=8] {'crop','rows'}, use_global_device_ids=true, to_apply=%region_11.13 | all-reduce | flops 18432 | bytes 73728 | tf_op jit(solution)/shard_map/psum | solution.py:89
  353.5 0.7 convert_element_type.95
  354.2 1.0 convert_element_type.92
  355.2 0.9 slice_bitcast_fusion
  356.1 17.5 %reduce-scatter.3.cloned.1.call-done = bf16[1,2,64,512]{3,2,1,0:T(8,128)(2,1)} async-done(((bf16[1,2,64,4096]{3,2,1,0:T(8,128)(2,1)}), bf16[1,2,64,512]{3,2,1,0:T(8,128)(2,1)}) %reduce-scatter.3.cloned.1.call-update) | async-done | bytes 131088 | tf_op jit(solution)/shard_map/reduce_scatter | solution.py:99
  (35 shorter events, 1.6 us)
Async XLA Ops:
  7.2 44.3 %all-gather.9.cloned.1.call-start = ((), (), s32[]{:S(2)}) async-start(), calls=%async_computation.4 | async-start | bytes 1179648 | tf_op jit(solution)/shard_map/all_gather | solution.py:40
  7.9 82.5 %all-gather.5.cloned.1.call-start = ((), (), s32[]{:S(2)}) async-start(), calls=%async_computation.2 | async-start | bytes 1179648 | tf_op jit(solution)/shard_map/all_gather | solution.py:41
  8.6 123.2 %all-gather.7.cloned.1.call-start = ((), (), s32[]{:S(2)}) async-start(), calls=%async_computation.3 | async-start | bytes 5570560 | tf_op jit(solution)/shard_map/all_gather | solution.py:37
  10.5 167.7 %all-gather.11.cloned.1.call-start = ((), (), s32[]{:S(2)}) async-start(), calls=%async_computation.5 | async-start | bytes 5570560 | tf_op jit(solution)/shard_map/all_gather | solution.py:36
  12.3 341.8 %reduce-scatter.5.cloned.1.call-start = ((), (), s32[]{:S(2)}) async-start(), calls=%async_computation.7 | async-start | bytes 10813440 | tf_op jit(solution)/shard_map/reduce_scatter | solution.py:108
  101.6 34.5 %copy-start = (bf16[40,128,256]{2,1,0:T(8,128)(2,1)}, bf16[40,128,256]{2,1,0:T(8,128)(2,1)S(1)}, u32[]{:S(2)}) copy-start(bf16[40,128,256]{2,1,0:T(8,128)(2,1)S(1)} %get-tuple-element.43) | copy-start | bytes 7864324
  136.1 8.0 %copy-start.5 = (f32[9,2048]{1,0:T(8,128)S(1)}, f32[9,2048]{1,0:T(8,128)}, u32[]{:S(2)}) copy-start(f32[9,2048]{1,0:T(8,128)} %param.12) | copy-start | bytes 221188
  138.6 7.7 %collective-permute-start = (bf16[1,1,64,2048]{3,2,1,0:T(8,128)(2,1)S(1)}, bf16[1,1,64,2048]{3,2,1,0:T(8,128)(2,1)S(1)}, u32[]{:S(2)}, u32[]{:S(2)}) collective-permute-start(bf16[1,1,64,2048]{3,2,1,0:T(8,128)(2,1)S(1)} %get-tuple-element.32), channel_id=1, source_target_pairs={{0,8},{8,16},{16,24},{24,32},{32,40},{40,48},{48,56},{56,64},{64,7... | collective-permute-start | bytes 786440 | tf_op jit(solution)/shard_map/ppermute | solution.py:18
  140.7 9.2 %collective-permute-start.1 = (bf16[1,1,64,2048]{3,2,1,0:T(8,128)(2,1)S(1)}, bf16[1,1,64,2048]{3,2,1,0:T(8,128)(2,1)S(1)}, u32[]{:S(2)}, u32[]{:S(2)}) collective-permute-start(bf16[1,1,64,2048]{3,2,1,0:T(8,128)(2,1)S(1)} %get-tuple-element.33), channel_id=1, source_target_pairs={{8,0},{16,8},{24,16},{32,24},{40,32},{48,40},{56,48},{64,56},{72,6... | collective-permute-start | bytes 786440 | tf_op jit(solution)/shard_map/ppermute | solution.py:19
  150.0 28.1 %copy-start.2 = (bf16[40,128,256]{2,1,0:T(8,128)(2,1)S(1)}, bf16[40,128,256]{2,1,0:T(8,128)(2,1)}, u32[]{:S(2)}) copy-start(bf16[40,128,256]{2,1,0:T(8,128)(2,1)} %get-tuple-element.44) | copy-start | bytes 7864324
  187.5 8.4 %collective-permute-start.2 = (bf16[1,1,64,2048]{3,2,1,0:T(8,128)(2,1)S(1)}, bf16[1,1,64,2048]{3,2,1,0:T(8,128)(2,1)S(1)}, u32[]{:S(2)}, u32[]{:S(2)}) collective-permute-start(bf16[1,1,64,2048]{3,2,1,0:T(8,128)(2,1)S(1)} %get-tuple-element.30), channel_id=1, source_target_pairs={{0,8},{8,16},{16,24},{24,32},{32,40},{40,48},{48,56},{56,64},{64,7... | collective-permute-start | bytes 786440 | tf_op jit(solution)/shard_map/ppermute | solution.py:18
  189.7 7.3 %collective-permute-start.3 = (bf16[1,1,64,2048]{3,2,1,0:T(8,128)(2,1)S(1)}, bf16[1,1,64,2048]{3,2,1,0:T(8,128)(2,1)S(1)}, u32[]{:S(2)}, u32[]{:S(2)}) collective-permute-start(bf16[1,1,64,2048]{3,2,1,0:T(8,128)(2,1)S(1)} %get-tuple-element.31), channel_id=1, source_target_pairs={{8,0},{16,8},{24,16},{32,24},{40,32},{48,40},{56,48},{64,56},{72,6... | collective-permute-start | bytes 786440 | tf_op jit(solution)/shard_map/ppermute | solution.py:19
  193.3 3.7 copy-start.3
  197.2 1.7 copy-start.1
  221.6 0.7 copy-start.6
  221.6 1.1 copy-start.4
  221.6 152.0 %reduce-scatter.3.cloned.1.call-start = ((), (), s32[]{:S(2)}) async-start(), calls=%async_computation.6 | async-start | bytes 1179648 | tf_op jit(solution)/shard_map/reduce_scatter | solution.py:99
Sparse Core Ops, SparseCore 0:
  9.8 41.6 all-gather.8
  53.3 37.0 all-gather.4
  92.8 39.0 all-gather.6
  134.0 44.0 all-gather.10
  221.7 110.2 reduce-scatter.4
  335.1 38.3 reduce-scatter.2
where the time goes:
time: 381 us; the launch traced here: 380 us
  waiting for transfers between devices  157 us (41%)
  blocking collectives  117 us (31%)
  local copies, waits for them, and re-layouts  41.1 us (11%)
  matrix products  23.8 us (6%)
  other arithmetic  15.2 us (4%)
  between operations  14.3 us (4%)
  starting transfers between devices  11.8 us (3%)
    psum x1, blocking collectives, on_device(): lax.psum(kern_local.astype(jnp.bfloat16), ('crop', 'rows'))  117 us
    all_gather x1, waiting for transfers between devices, on_device(): lax.all_gather(tokens, 'hid', axis=3, tiled=True)  38.3 us
    all_gather x1, waiting for transfers between devices, on_device(): lax.all_gather(cotangent, 'hid', axis=3, tiled=True)  37.1 us
    all_gather x1, waiting for transfers between devices, on_device(): lax.all_gather(weight_out, 'rows', axis=0, tiled=True)  30.2 us
    all_gather x1, waiting for transfers between devices, on_device(): lax.all_gather(weight_in, 'rows', axis=0, tiled=True)  25.9 us
    reduce_scatter x1, waiting for transfers between devices, on_device(): lax.psum_scatter(token_terms.astype(jnp.bfloat16), 'hid', scatter_dimensi...  17.5 us
    convert_element_type x1, local copies, waits for them, and re-layouts, on_device(): (jnp.stack([first_term, second_term], axis=1) * loss_scale).astype(jnp.bf...  15.4 us
    unnamed x21, local copies, waits for them, and re-layouts  9.42 us
  transfers between devices with their start and end apart: 10, of which 8 were waited for; matrix products, arithmetic and copies ran while one was open for 12% of the time, Pallas kernels for 0%

commit v1 on v0

--- a/solution.py
+++ b/solution.py
@@ -37,7 +37,9 @@
         lax.all_gather(weight_out, "rows", axis=0, tiled=True),
     )
     tok_full, cot_full = (
-        lax.all_gather(tokens, "hid", axis=3, tiled=True),
+        jnp.concatenate(
+            lax.all_to_all(jnp.stack([tokens] * lax.axis_size("hid")), "hid", 0, 0), axis=3
+        ),
         lax.all_gather(cotangent, "hid", axis=3, tiled=True),
     )
     crop_count, height, grid_width, depth_all = tok_full.shape

time: 381 us -> 352 us (0.924)
  waiting for transfers between devices: 157 us -> 117 us
  starting transfers between devices: 11.8 us -> 20 us
    all_gather x1 -> x0, waiting for transfers between devices: 38.3 us -> none  [on_device(): lax.all_gather(tokens, 'hid', axis=3, tiled=True)]
    all_to_all x0 -> x1, starting transfers between devices: none -> 8.47 us  [on_device(): lax.all_to_all(jnp.stack([tokens] * lax.axis_size('hid')), 'hid', 0, 0)]
    another operation x0 -> x3, local copies, waits for them, and re-layouts: none -> 4.78 us  [the longest x2 2.77 us: on_device(): tok_full.reshape(tok_count, block_count, block_size)]
    unnamed x21 -> x20, local copies, waits for them, and re-layouts: 9.42 us -> 8.16 us
  transfers between devices with their start and end apart: 10 -> 10, of which waited for: 8 -> 7; matrix products, arithmetic and copies ran while one was open for 12% -> 14% of each run, Pallas kernels for 0% -> 0%
where the time goes in v1:
time: 352 us; the launch traced here: 351 us
  waiting for transfers between devices  117 us (33%)
  blocking collectives  117 us (33%)
  local copies, waits for them, and re-layouts  44.1 us (13%)
  matrix products  23.8 us (7%)
  starting transfers between devices  20 us (6%)
  other arithmetic  15.1 us (4%)
  between operations  14 us (4%)
    psum x1, blocking collectives, on_device(): lax.psum(kern_local.astype(jnp.bfloat16), ('crop', 'rows'))  117 us
    all_gather x1, waiting for transfers between devices, on_device(): lax.all_gather(cotangent, 'hid', axis=3, tiled=True)  38 us
    all_gather x1, waiting for transfers between devices, on_device(): lax.all_gather(weight_out, 'rows', axis=0, tiled=True)  28.2 us
    all_gather x1, waiting for transfers between devices, on_device(): lax.all_gather(weight_in, 'rows', axis=0, tiled=True)  26.4 us
    reduce_scatter x1, waiting for transfers between devices, on_device(): lax.psum_scatter(token_terms.astype(jnp.bfloat16), 'hid', scatter_dimensi...  17.5 us
    convert_element_type x1, local copies, waits for them, and re-layouts, on_device(): (jnp.stack([first_term, second_term], axis=1) * loss_scale).astype(jnp.bf...  15.4 us
    all_to_all x1, starting transfers between devices, on_device(): lax.all_to_all(jnp.stack([tokens] * lax.axis_size('hid')), 'hid', 0, 0)  8.47 us
    unnamed x20, local copies, waits for them, and re-layouts  8.16 us
  transfers between devices with their start and end apart: 10, of which 7 were waited for; matrix products, arithmetic and copies ran while one was open for 14% of the time, Pallas kernels for 0%

profile of v1, /device:TPU:4, one launch (start us, length us, event | category | flops | bytes accessed | tf_op | source)
XLA Modules:
  0.0 351.3 jit_solution(7625391671693953295)
XLA Ops:
  7.2 0.7 all-gather.4.cloned.1.call-update
  8.0 1.8 copy.46
  9.8 1.8 copy.50
  11.6 2.0 stack.50
  13.6 8.5 %all-to-all-start = ((bf16[8,1,2,64,512]{4,3,2,1,0:T(8,128)(2,1)}), bf16[8,1,2,64,512]{4,3,2,1,0:T(8,128)(2,1)S(1)}, u32[]{:S(2)}, u32[]{:S(2)}) async-start(bf16[8,1,2,64,512]{4,3,2,1,0:T(8,128)(2,1)} %stack.50), calls=%async_computation | async-start | bytes 2097152 | tf_op jit(solution)/shard_map/all_to_all | solution.py:41
  22.2 38.0 %all-gather.4.cloned.1.call-done = bf16[1,2,64,4096]{3,2,1,0:T(8,128)(2,1)} async-done(((bf16[1,2,64,512]{3,2,1,0:T(8,128)(2,1)}), bf16[1,2,64,4096]{3,2,1,0:T(8,128)(2,1)}) %all-gather.4.cloned.1.call-update) | async-done | bytes 1048592 | tf_op jit(solution)/shard_map/all_gather | solution.py:43
  60.2 1.5 copy.69
  61.7 0.3 copy.45
  62.0 0.6 copy.48
  62.6 1.2 reshape_reshape.3
  63.8 1.6 copy.49
  65.4 2.4 gather_fusion.1
  67.8 2.4 gather_fusion
  70.2 4.6 %broadcast_select_fusion.1 = (bf16[40,128,256]{2,1,0:T(8,128)(2,1)S(1)}, bf16[40,128,256]{2,1,0:T(8,128)(2,1)}) fusion(bf16[40,128,256]{2,1,0:T(8,128)(2,1)} %gather_fusion, pred[40]{0:T(512)(128)(4,1)S(1)} %compare_and_fusion, bf16[40,128,256]{2,1,0:T(8,128)(2,1)} %gather_fusion.1), kind=kLoop, calls=%fused_computation.18 | loop fusion | flops 2621440 | bytes 10485800 | tf_op jit(solution)/shard_map/jit(_take)/select_n | solution.py:56
  74.8 28.2 %all-gather.6.cloned.1.call-done = bf16[256,8,5,256]{3,0,2,1:T(8,128)(2,1)} async-done(((bf16[16,8,5,256]{3,0,2,1:T(8,128)(2,1)}), bf16[256,8,5,256]{3,0,2,1:T(8,128)(2,1)}) %all-gather.6.cloned.1.call-update) | async-done | bytes 5242896 | tf_op jit(solution)/shard_map/all_gather | solution.py:37
  103.0 4.3 %fusion.9 = bf16[128,8,256]{2,0,1:T(8,128)(2,1)S(1)} fusion(bf16[128,8,5,256]{3,0,2,1:T(8,128)(2,1)S(1)} %bitcast.97, bf16[256,8,5,256]{3,0,2,1:T(8,128)(2,1)} %all-gather.6.cloned.1.call-done), kind=kOutput, calls=%fused_computation.39 | convolution fusion | flops 671350784 | bytes 8388608 | tf_op jit(solution)/shard_map/tckd,fckd->tcf/dot_general | solution.py:64
  107.4 1.1 copy.47
  108.4 1.3 reshape.188
  109.8 2.1 collective-permute-start
  111.9 3.4 collective-permute-start.1
  115.4 2.0 collective-permute-done
  117.5 3.3 collective-permute-done.1
  120.9 0.9 fusion.25
  121.8 1.3 copy.70
  123.1 26.4 %all-gather.8.cloned.1.call-done = bf16[256,8,5,256]{3,0,2,1:T(8,128)(2,1)} async-done(((bf16[16,8,5,256]{3,0,2,1:T(8,128)(2,1)}), bf16[256,8,5,256]{3,0,2,1:T(8,128)(2,1)}) %all-gather.8.cloned.1.call-update) | async-done | bytes 5242896 | tf_op jit(solution)/shard_map/all_gather | solution.py:36
  149.5 5.1 %multiply_convert_fusion = (bf16[128,8,256]{2,0,1:T(8,128)(2,1)S(1)}, bf16[128,8,256]{2,0,1:T(8,128)(2,1)}) fusion(f32[128,8,256]{2,1,0:T(8,128)} %bitcast.107, bf16[128,8,5,256]{3,0,2,1:T(8,128)(2,1)S(1)} %bitcast.99, bf16[256,8,5,256]{3,0,2,1:T(8,128)(2,1)} %all-gather.8.cloned.1.call-done), kind=kOutput, calls=%fused_computation.76 | convolution fusion | flops 676593664 | bytes 9961472 | tf_op jit(solution)/shard_map/tckb,bcke->tce/dot_general | solution.py:59
  154.7 1.1 copy.54
  155.7 2.1 reshape.192
  157.8 1.1 fusion.46
  158.9 2.1 collective-permute-start.2
  161.1 3.6 %collective-permute-start.3 = (bf16[1,1,64,2048]{3,2,1,0:T(8,128)(2,1)S(1)}, bf16[1,1,64,2048]{3,2,1,0:T(8,128)(2,1)S(1)}, u32[]{:S(2)}, u32[]{:S(2)}) collective-permute-start(bf16[1,1,64,2048]{3,2,1,0:T(8,128)(2,1)S(1)} %get-tuple-element.31), channel_id=1, source_target_pairs={{8,0},{16,8},{24,16},{32,24},{40,32},{48,40},{56,48},{64,56},{72,6... | collective-permute-start | bytes 786440 | tf_op jit(solution)/shard_map/ppermute | solution.py:19
  164.7 2.7 convolution_bitcast_fusion.1
  167.3 1.0 collective-permute-done.3
  168.5 0.9 add_convert_fusion
  169.5 0.7 copy-done.1
  170.3 1.6 convolution_bitcast_fusion
  171.8 5.7 %fusion = bf16[256,2,8,5,256]{0,4,3,2,1:T(8,128)(2,1)} fusion(f32[256,1,8,5,256]{0,4,3,2,1:T(8,128)S(1)} %convolution_bitcast_fusion, f32[256,1,8,5,256]{0,4,3,2,1:T(8,128)S(1)} %convolution_bitcast_fusion.1), kind=kLoop, calls=%fused_computation.3 | loop fusion | flops 15728640 | bytes 31457280 | tf_op jit(solution)/shard_map/convert_element_type | solution.py:111
  177.5 15.4 %copy.57 = bf16[256,2,8,5,256]{4,2,3,1,0:T(8,128)(2,1)} copy(bf16[256,2,8,5,256]{0,4,3,2,1:T(8,128)(2,1)} %fusion) | data formatting | bytes 20971520 | tf_op jit(solution)/shard_map/convert_element_type | solution.py:111
  193.0 0.9 copy-done.4
  193.9 4.3 %convolution_bitcast_fusion.2 = f32[128,8,5,256]{3,0,2,1:T(8,128)S(1)} fusion(bf16[256,8,5,256]{3,0,2,1:T(8,128)(2,1)} %all-gather.8.cloned.1.call-done, bf16[128,8,256]{2,0,1:T(8,128)(2,1)S(1)} %copy-done.4), kind=kOutput, calls=%fused_computation.19 | convolution fusion | flops 671088640 | bytes 11010048 | tf_op jit(solution)/shard_map/tce,bcke->tckb/dot_general | solution.py:92
  198.2 5.8 %fusion.5 = bf16[128,16,256]{2,1,0:T(8,128)(2,1)} fusion(f32[128,8,5,256]{3,0,2,1:T(8,128)S(1)} %convolution_bitcast_fusion.2, s32[8,5]{0,1:T(8,128)S(1)} %copy.44), kind=kOutput, calls=%fused_computation.35 | convolution fusion | flops 252183168 | bytes 6291616 | tf_op jit(solution)/shard_map/tckb,ckr->trb/dot_general | solution.py:98
  204.0 2.3 convert_element_type.87
  206.4 1.0 fusion.39
  207.6 117.1 %psum.7 = bf16[9,2048]{1,0:T(8,128)(2,1)S(1)} all-reduce(bf16[9,2048]{1,0:T(8,128)(2,1)S(1)} %multiply_convert_fusion.1), channel_id=1, replica_groups=mesh['crop'=2,'rows'=16,'hid'=8] {'crop','rows'}, use_global_device_ids=true, to_apply=%region_11.13 | all-reduce | flops 18432 | bytes 73728 | tf_op jit(solution)/shard_map/psum | solution.py:91
  324.7 0.7 convert_element_type.95
  325.4 1.0 convert_element_type.92
  326.4 0.9 slice_bitcast_fusion
  327.3 17.5 %reduce-scatter.3.cloned.1.call-done = bf16[1,2,64,512]{3,2,1,0:T(8,128)(2,1)} async-done(((bf16[1,2,64,4096]{3,2,1,0:T(8,128)(2,1)}), bf16[1,2,64,512]{3,2,1,0:T(8,128)(2,1)}) %reduce-scatter.3.cloned.1.call-update) | async-done | bytes 131088 | tf_op jit(solution)/shard_map/reduce_scatter | solution.py:101
  (36 shorter events, 1.2 us)
Async XLA Ops:
  7.2 53.0 %all-gather.4.cloned.1.call-start = ((), (), s32[]{:S(2)}) async-start(), calls=%async_computation.3 | async-start | bytes 1179648 | tf_op jit(solution)/shard_map/all_gather | solution.py:43
  7.9 14.2 %copy-start.6 = (s32[8,5]{1,0:T(8,128)S(1)}, s32[8,5]{1,0:T(8,128)}, u32[]{:S(2)}) copy-start(s32[8,5]{1,0:T(8,128)} %param.13) | copy-start | bytes 484
  7.9 95.1 %all-gather.6.cloned.1.call-start = ((), (), s32[]{:S(2)}) async-start(), calls=%async_computation.4 | async-start | bytes 5570560 | tf_op jit(solution)/shard_map/all_gather | solution.py:37
  9.7 139.8 %all-gather.8.cloned.1.call-start = ((), (), s32[]{:S(2)}) async-start(), calls=%async_computation.5 | async-start | bytes 5570560 | tf_op jit(solution)/shard_map/all_gather | solution.py:36
  13.6 48.4 %all-to-all-start = ((bf16[8,1,2,64,512]{4,3,2,1,0:T(8,128)(2,1)}), bf16[8,1,2,64,512]{4,3,2,1,0:T(8,128)(2,1)S(1)}, u32[]{:S(2)}, u32[]{:S(2)}) async-start(bf16[8,1,2,64,512]{4,3,2,1,0:T(8,128)(2,1)} %stack.50), calls=%async_computation | async-start | bytes 2097152 | tf_op jit(solution)/shard_map/all_to_all | solution.py:41
  22.0 303.4 %reduce-scatter.5.cloned.1.call-start = ((), (), s32[]{:S(2)}) async-start(), calls=%async_computation.7 | async-start | bytes 10813440 | tf_op jit(solution)/shard_map/reduce_scatter | solution.py:110
  74.8 32.5 %copy-start = (bf16[40,128,256]{2,1,0:T(8,128)(2,1)}, bf16[40,128,256]{2,1,0:T(8,128)(2,1)S(1)}, u32[]{:S(2)}) copy-start(bf16[40,128,256]{2,1,0:T(8,128)(2,1)S(1)} %get-tuple-element.43) | copy-start | bytes 7864324
  107.3 8.0 %copy-start.5 = (f32[9,2048]{1,0:T(8,128)S(1)}, f32[9,2048]{1,0:T(8,128)}, u32[]{:S(2)}) copy-start(f32[9,2048]{1,0:T(8,128)} %param.12) | copy-start | bytes 221188
  109.8 7.7 %collective-permute-start = (bf16[1,1,64,2048]{3,2,1,0:T(8,128)(2,1)S(1)}, bf16[1,1,64,2048]{3,2,1,0:T(8,128)(2,1)S(1)}, u32[]{:S(2)}, u32[]{:S(2)}) collective-permute-start(bf16[1,1,64,2048]{3,2,1,0:T(8,128)(2,1)S(1)} %get-tuple-element.32), channel_id=1, source_target_pairs={{0,8},{8,16},{16,24},{24,32},{32,40},{40,48},{48,56},{56,64},{64,7... | collective-permute-start | bytes 786440 | tf_op jit(solution)/shard_map/ppermute | solution.py:18
  111.9 8.8 %collective-permute-start.1 = (bf16[1,1,64,2048]{3,2,1,0:T(8,128)(2,1)S(1)}, bf16[1,1,64,2048]{3,2,1,0:T(8,128)(2,1)S(1)}, u32[]{:S(2)}, u32[]{:S(2)}) collective-permute-start(bf16[1,1,64,2048]{3,2,1,0:T(8,128)(2,1)S(1)} %get-tuple-element.33), channel_id=1, source_target_pairs={{8,0},{16,8},{24,16},{32,24},{40,32},{48,40},{56,48},{64,56},{72,6... | collective-permute-start | bytes 786440 | tf_op jit(solution)/shard_map/ppermute | solution.py:19
  120.9 28.6 %copy-start.2 = (bf16[40,128,256]{2,1,0:T(8,128)(2,1)S(1)}, bf16[40,128,256]{2,1,0:T(8,128)(2,1)}, u32[]{:S(2)}) copy-start(bf16[40,128,256]{2,1,0:T(8,128)(2,1)} %get-tuple-element.44) | copy-start | bytes 7864324
  158.9 8.4 %collective-permute-start.2 = (bf16[1,1,64,2048]{3,2,1,0:T(8,128)(2,1)S(1)}, bf16[1,1,64,2048]{3,2,1,0:T(8,128)(2,1)S(1)}, u32[]{:S(2)}, u32[]{:S(2)}) collective-permute-start(bf16[1,1,64,2048]{3,2,1,0:T(8,128)(2,1)S(1)} %get-tuple-element.30), channel_id=1, source_target_pairs={{0,8},{8,16},{16,24},{24,32},{32,40},{40,48},{48,56},{56,64},{64,7... | collective-permute-start | bytes 786440 | tf_op jit(solution)/shard_map/ppermute | solution.py:18
  161.1 7.3 %collective-permute-start.3 = (bf16[1,1,64,2048]{3,2,1,0:T(8,128)(2,1)S(1)}, bf16[1,1,64,2048]{3,2,1,0:T(8,128)(2,1)S(1)}, u32[]{:S(2)}, u32[]{:S(2)}) collective-permute-start(bf16[1,1,64,2048]{3,2,1,0:T(8,128)(2,1)S(1)} %get-tuple-element.31), channel_id=1, source_target_pairs={{8,0},{16,8},{24,16},{32,24},{40,32},{48,40},{56,48},{64,56},{72,6... | collective-permute-start | bytes 786440 | tf_op jit(solution)/shard_map/ppermute | solution.py:19
  164.7 3.7 %copy-start.3 = (bf16[1,2,64,2048]{3,2,1,0:T(8,128)(2,1)S(1)}, bf16[1,2,64,2048]{3,2,1,0:T(8,128)(2,1)}, u32[]{:S(2)}) copy-start(bf16[1,2,64,2048]{3,2,1,0:T(8,128)(2,1)} %reshape.192) | copy-start | bytes 1572868
  168.5 1.7 copy-start.1
  192.8 1.0 copy-start.4
  192.9 151.9 %reduce-scatter.3.cloned.1.call-start = ((), (), s32[]{:S(2)}) async-start(), calls=%async_computation.6 | async-start | bytes 1179648 | tf_op jit(solution)/shard_map/reduce_scatter | solution.py:101
Sparse Core Ops, SparseCore 0:
  9.8 50.3 all-gather.3
  62.6 40.4 all-gather.5
  105.4 44.0 all-gather.7
  193.0 110.1 reduce-scatter.4
  306.4 38.3 reduce-scatter.2
